TPU v7x, 512 devices: a whole 4x4x16 slice. The times are simulated.
512 devices in a mesh: ctx: 32 (over x, y, core), head: 16 (over z).
Axes of the slice: x: 4, y: 4, z: 16, core: 2. Of those that a mesh axis runs over, the one named last changes fastest.
Arguments:
- mixed_in: bfloat16 [8192, 8192], P(('ctx', 'head')), may hold values from -6 to 6
- conv_weight: float32 [4, 8192], P(None, 'head'), may hold values from -3 to 3
- write_strength_logit: float32 [32, 8192], P('head', 'ctx'), may hold values from -10.5 to 2.2, as said below
- decay_log: float32 [32, 8192], P('head', 'ctx'), may hold values from -0.7 to 0, as said below
- initial_state: float32 [32, 128, 128], P('head'), may hold values from -6 to 6
- final_state_grad: float32 [32, 128, 128], P('head'), may hold values from -6 to 6
- grad_out: bfloat16 [8192, 4096], P('ctx', 'head'), may hold values from -6 to 6
Outputs:
- grad_mixed: bfloat16 [8192, 8192], P(('ctx', 'head'))
- grad_conv: float32 [4, 8192], P(None, 'head')
- grad_beta_logit: float32 [32, 8192], P('head', 'ctx')
- grad_decay_log: float32 [32, 8192], P('head', 'ctx')
Inputs may be any that keep to these rules, and one draw needn't show every extreme that they name: `write_strength_logit`: each value head's write strengths and decays vary from token to token. `decay_log`: every entry is negative.
All inputs are finite; a program needn't handle non-finite values.
Results may differ from a plain program's by a relative error of at most 0.001.
Values may be sent and summed in bfloat16 or wider, within the bound.
A program may use at most 64 MiB of HBM per device.

v0:
```python
import jax
import jax.numpy as jnp
from jax import lax
from jax.sharding import PartitionSpec as P

HK = 16
VALUE_HEADS = 32
DK = 128
DV = 128
KW = 4
BLOCK = 64
highest = lax.Precision.HIGHEST
norm_eps = 1e-06


def from_behind(value, axis, by):
    devices = lax.axis_size(axis)
    pairs = [(i, i + by) for i in range(devices) if 0 <= i + by < devices]
    return lax.ppermute(value, axis, pairs)


def prefix(value, axis, combine, identity, reverse):
    devices, mine = (lax.axis_size(axis), lax.axis_index(axis))
    everything = jax.tree.map(lambda part: lax.all_gather(part, axis), value)
    start = jax.tree.map(
        lambda part, zero: jnp.broadcast_to(jnp.asarray(zero, part.dtype), part.shape),
        value,
        identity,
    )

    def step(k, before):
        at = devices - 1 - k if reverse else k
        reached = at > mine if reverse else at < mine
        new = combine(before, jax.tree.map(lambda part: part[at], everything))
        return jax.tree.map(lambda a, b: jnp.where(reached, a, b), new, before)

    return lax.fori_loop(0, devices, step, start)


def block_step(carried, pieces):
    state, transit = carried
    queries, key_feats, values, beta_gate, log_decay = pieces
    block_size = log_decay.shape[0]
    cumulative = jnp.cumsum(log_decay)
    row_ids = lax.broadcasted_iota(jnp.int32, (block_size, block_size), 0)
    col_ids = lax.broadcasted_iota(jnp.int32, (block_size, block_size), 1)
    causal = col_ids <= row_ids
    differ = jnp.where(causal, cumulative[:, None] - cumulative[None, :], 0.0)
    ratios = jnp.where(causal, jnp.exp(differ), 0.0)
    key_gram = jnp.dot(key_feats, key_feats.T, precision=highest)
    lower_part = jnp.where(col_ids < row_ids, beta_gate[:, None] * ratios * key_gram, 0.0)
    system = lower_part + jnp.eye(block_size, dtype=jnp.float32)
    decays = jnp.exp(cumulative)
    right_sides = jnp.concatenate(
        [beta_gate[:, None] * values, (beta_gate * decays)[:, None] * key_feats], axis=1
    )
    solved = jax.scipy.linalg.solve_triangular(system, right_sides, lower=True)
    width_v = values.shape[1]
    base_update = solved[:, :width_v]
    weights = solved[:, width_v:]
    update = base_update - jnp.dot(weights, state, precision=highest)
    scores = ratios * jnp.dot(queries, key_feats.T, precision=highest)
    output = decays[:, None] * jnp.dot(queries, state, precision=highest) + jnp.dot(
        scores, update, precision=highest
    )
    total_decay = jnp.exp(cumulative[-1])
    tail_keys = jnp.exp(cumulative[-1] - cumulative)[:, None] * key_feats
    new_state = total_decay * state + jnp.dot(tail_keys.T, update, precision=highest)
    step_map = total_decay * jnp.eye(key_feats.shape[1], dtype=jnp.float32) - jnp.dot(
        tail_keys.T, weights, precision=highest
    )
    new_transit = jnp.dot(step_map, transit, precision=highest)
    return ((new_state, new_transit), output)


def run_head(state, queries, key_feats, values, beta_gate, log_decay):
    blocks = queries.shape[0] // BLOCK
    pieces = (
        queries.reshape(blocks, BLOCK, -1),
        key_feats.reshape(blocks, BLOCK, -1),
        values.reshape(blocks, BLOCK, -1),
        beta_gate.reshape(blocks, BLOCK),
        log_decay.reshape(blocks, BLOCK),
    )
    start = (state, jnp.eye(key_feats.shape[1], dtype=jnp.float32))
    (state_end, transit), outputs = lax.scan(block_step, start, pieces)
    return (outputs.reshape(-1, values.shape[1]), state_end, transit)


def normalize(feats, factor):
    return feats * lax.rsqrt(jnp.sum(feats * feats, axis=-1, keepdims=True) + norm_eps) * factor


def mix_layer(state_in, extended, conv_weight, write_strength_logit, decay_log):
    row_count = extended.shape[0] - (KW - 1)
    filtered_signal = conv_weight[0] * extended[0:row_count]
    for tap in range(1, KW):
        filtered_signal = filtered_signal + conv_weight[tap] * extended[tap : tap + row_count]
    activated = jax.nn.silu(filtered_signal)
    ratio_heads = VALUE_HEADS // HK
    group_width = 2 * DK + ratio_heads * DV
    groups = activated.reshape(row_count, -1, group_width)
    key_heads = groups.shape[1]
    queries = normalize(groups[:, :, :DK], DK ** (-0.5))
    key_feats = normalize(groups[:, :, DK : 2 * DK], 1.0)
    values = (
        groups[:, :, 2 * DK :].reshape(row_count, key_heads * ratio_heads, DV).transpose(1, 0, 2)
    )
    queries = jnp.repeat(queries.transpose(1, 0, 2), ratio_heads, axis=0)
    key_feats = jnp.repeat(key_feats.transpose(1, 0, 2), ratio_heads, axis=0)
    beta_gate = jax.nn.sigmoid(write_strength_logit)
    outputs, state_out, transit = jax.vmap(run_head)(
        state_in, queries, key_feats, values, beta_gate, decay_log
    )
    result = outputs.transpose(1, 0, 2).reshape(row_count, -1)
    return ((result, state_out), transit)


def compose(earlier, later):
    matrix = jnp.einsum("hij,hjk->hik", later[0], earlier[0], precision=highest)
    offset = jnp.einsum("hij,hjk->hik", later[0], earlier[1], precision=highest) + later[1]
    return (matrix, offset)


def advance(maps, state):
    return jnp.einsum("hij,hjk->hik", maps[0], state, precision=highest) + maps[1]


def on_device(
    mixed_in,
    conv_weight,
    write_strength_logit,
    decay_log,
    initial_state,
    final_state_grad,
    grad_out,
):
    local_in = lax.all_to_all(mixed_in, "head", split_axis=1, concat_axis=0, tiled=True)
    edge_rows = from_behind(local_in[-(KW - 1) :], "ctx", 1)
    extended = jnp.concatenate([edge_rows, local_in], axis=0).astype(jnp.float32)
    cotangent = grad_out.astype(jnp.float32)
    zeros_state = jnp.zeros_like(initial_state)

    def from_state(state):
        return mix_layer(state, extended, conv_weight, write_strength_logit, decay_log)

    primal, pull_state, transit = jax.vjp(from_state, zeros_state, has_aux=True)
    offset = primal[1]
    local_grad = pull_state((cotangent, jnp.zeros_like(offset)))[0]
    flipped = jnp.swapaxes(transit, 1, 2)
    identity = (
        jnp.broadcast_to(jnp.eye(transit.shape[1], dtype=jnp.float32), transit.shape),
        jnp.zeros_like(offset),
    )
    earlier_map = prefix((transit, offset), "ctx", compose, identity, False)
    later_map = prefix((flipped, local_grad), "ctx", compose, identity, True)
    state_in = advance(earlier_map, initial_state)
    state_grad = advance(later_map, final_state_grad)

    def forward(ext_rows, weight_taps, logits, decay_logs):
        return mix_layer(state_in, ext_rows, weight_taps, logits, decay_logs)

    unused, pull_all, unused_transit = jax.vjp(
        forward, extended, conv_weight, write_strength_logit, decay_log, has_aux=True
    )
    grad_ext, grad_weight, grad_beta, grad_decay = pull_all((cotangent, state_grad))
    spilled = from_behind(grad_ext[: KW - 1], "ctx", -1)
    own_grad = grad_ext[KW - 1 :]
    own_grad = jnp.concatenate([own_grad[: -(KW - 1)], own_grad[-(KW - 1) :] + spilled], axis=0)
    returned = lax.all_to_all(
        own_grad.astype(jnp.bfloat16), "head", split_axis=0, concat_axis=1, tiled=True
    )
    weight_total = lax.psum(grad_weight, "ctx")
    return (returned, weight_total, grad_beta, grad_decay)


def solution(mesh):
    in_specs = (
        P(("ctx", "head"), None),
        P(None, "head"),
        P("head", "ctx"),
        P("head", "ctx"),
        P("head", None, None),
        P("head", None, None),
        P("ctx", "head"),
    )
    out_specs = (P(("ctx", "head"), None), P(None, "head"), P("head", "ctx"), P("head", "ctx"))
    return jax.shard_map(
        on_device, mesh=mesh, in_specs=in_specs, out_specs=out_specs, check_vma=False
    )
```

profile of v0, /device:TPU:32, one launch (start us, length us, event | category | flops | bytes accessed | tf_op | source)
XLA Modules:
  0.0 795.1 jit_solution(5155768118002871086)
XLA Ops:
  7.2 1.7 copy.147
  8.9 15.2 %all-to-all-start = ((bf16[16,16,512]{2,0,1:T(8,128)(2,1)}), bf16[16,16,512]{2,0,1:T(8,128)(2,1)S(1)}, u32[]{:S(2)}, u32[]{:S(2)}) async-start(bf16[16,16,512]{2,0,1:T(8,128)(2,1)} %bitcast.435), calls=%async_computation | async-start | bytes 524288 | tf_op jit(solution)/shard_map/all_to_all | solution.py:138
  26.4 15.6 %all-to-all-done = bf16[16,16,512]{2,0,1:T(8,128)(2,1)S(1)} async-done(((bf16[16,16,512]{2,0,1:T(8,128)(2,1)}), bf16[16,16,512]{2,0,1:T(8,128)(2,1)S(1)}, u32[]{:S(2)}, u32[]{:S(2)}) %all-to-all-start) | async-done | bytes 262176 | tf_op jit(solution)/shard_map/all_to_all | solution.py:138
  48.5 65.6 %while.169 = (s32[]{:T(128)}, f32[2,128,128]{2,1,0:T(8,128)S(1)}, f32[2,128,128]{2,1,0:T(8,128)S(1)}, f32[4,2,64,128]{3,2,1,0:T(8,128)S(1)}, f32[4,2,64,1]{2,1,3...) while((s32[]{:T(128)}, f32[2,128,128]{2,1,0:T(8,128)S(1)}, ...), condition=%wide.region_4.6_spmd.clone.clone, body=%wide.region_2.5_spmd.clone.clone.sunk | while | flops 176640128 | bytes 2980628 | solution.py:86
  51.5 9.8 %custom-call.35 = f32[2,1,64,64]{2,3,1,0:T(8,128)S(1)} custom-call(f32[2,1,64,64]{3,2,1,0:T(8,128)S(1)} %fusion.420), custom_call_target="InvertDiagBlocksLowerTriangular" | custom-call | tf_op jit(solution)/shard_map/jvp(vmap())/while/body/eval_jaxpr/jit(_solve_triangular)/triangular_solve/custom-call.1 | solution.py:57
  67.9 9.8 %custom-call.35 = f32[2,1,64,64]{2,3,1,0:T(8,128)S(1)} custom-call(f32[2,1,64,64]{3,2,1,0:T(8,128)S(1)} %fusion.420), custom_call_target="InvertDiagBlocksLowerTriangular" | custom-call | tf_op jit(solution)/shard_map/jvp(vmap())/while/body/eval_jaxpr/jit(_solve_triangular)/triangular_solve/custom-call.1 | solution.py:57
  84.2 9.8 %custom-call.35 = f32[2,1,64,64]{2,3,1,0:T(8,128)S(1)} custom-call(f32[2,1,64,64]{3,2,1,0:T(8,128)S(1)} %fusion.420), custom_call_target="InvertDiagBlocksLowerTriangular" | custom-call | tf_op jit(solution)/shard_map/jvp(vmap())/while/body/eval_jaxpr/jit(_solve_triangular)/triangular_solve/custom-call.1 | solution.py:57
  100.7 9.8 %custom-call.35 = f32[2,1,64,64]{2,3,1,0:T(8,128)S(1)} custom-call(f32[2,1,64,64]{3,2,1,0:T(8,128)S(1)} %fusion.420), custom_call_target="InvertDiagBlocksLowerTriangular" | custom-call | tf_op jit(solution)/shard_map/jvp(vmap())/while/body/eval_jaxpr/jit(_solve_triangular)/triangular_solve/custom-call.1 | solution.py:57
  116.9 9.2 %while.166 = (s32[]{:T(128)}, f32[2,128,128]{2,1,0:T(8,128)S(1)}, f32[4,2,1,1]{1,3,2,0:T(1,128)S(1)}, f32[4,2,64,128]{3,2,1,0:T(8,128)S(1)}, f32[4,2,64,1]{2,1,3...) while((s32[]{:T(128)}, f32[2,128,128]{2,1,0:T(8,128)S(1)}, ...), condition=%wide.region_6.8_spmd.clone, body=%wide.region_5.7_spmd.clone.sunk | while | flops 88293376 | bytes 1316019 | solution.py:86
  128.2 45.1 %all-gather.9.cloned.1.call-done = f32[64,128,128]{2,1,0:T(8,128)} async-done(((f32[2,128,128]{2,1,0:T(8,128)}), f32[64,128,128]{2,1,0:T(8,128)}) %all-gather.9.cloned.1.call-update) | async-done | bytes 4194320 | tf_op jit(solution)/shard_map/all_gather | solution.py:24
  173.2 64.6 %all-gather.11.cloned.1.call-done = f32[64,128,128]{2,1,0:T(8,128)} async-done(((f32[2,128,128]{2,1,0:T(8,128)}), f32[64,128,128]{2,1,0:T(8,128)}) %all-gather.11.cloned.1.call-update) | async-done | bytes 4194320 | tf_op jit(solution)/shard_map/all_gather | solution.py:24
  237.9 80.1 %while.167 = (s32[]{:T(128)}, f32[2,128,128]{2,1,0:T(8,128)S(1)}, f32[2,128,128]{2,1,0:T(8,128)S(1)}, s32[]{:T(128)}, f32[32,2,128,128]{3,2,1,0:T(8,128)}, /*ind...) while((s32[]{:T(128)}, f32[2,128,128]{2,1,0:T(8,128)S(1)}, ...), condition=%wide.region_8.10_spmd.clone, body=%wide.region_7.9_spmd.clone.sunk | while | flops 100827144 | bytes 1706674 | solution.py:37
  318.0 47.8 %all-gather.15.cloned.1.call-done = f32[64,128,128]{2,1,0:T(8,128)} async-done(((f32[2,128,128]{2,1,0:T(8,128)}), f32[64,128,128]{2,1,0:T(8,128)}) %all-gather.15.cloned.1.call-update) | async-done | bytes 4194320 | tf_op jit(solution)/shard_map/all_gather | solution.py:24
  365.9 79.6 %while.168 = (s32[]{:T(128)}, f32[2,128,128]{2,1,0:T(8,128)S(1)}, f32[2,128,128]{2,1,0:T(8,128)S(1)}, s32[]{:T(128)}, f32[32,2,128,128]{3,2,1,0:T(8,128)}, /*ind...) while((s32[]{:T(128)}, f32[2,128,128]{2,1,0:T(8,128)S(1)}, f32[2,128,128]{2,1,0:T(8,128)S(1)}, ...), condition=%wide.region_10.12_spmd.clone, body=%wide.region_9.11_spmd.clone.sunk | while | flops 100827136 | bytes 1706612 | solution.py:37
  458.0 107.3 %while.164 = (s32[]{:T(128)}, f32[2,128,128]{2,1,0:T(8,128)S(1)}, f32[4,2,64,64]{3,2,1,0:T(8,128)}, f32[4,2,128,64]{2,3,1,0:T(8,128)}, f32[4,2,64,64]{3,2,1,0:T(...) while((s32[]{:T(128)}, f32[2,128,128]{2,1,0:T(8,128)S(1)}, ...), condition=%wide.region_13.15_spmd.clone.clone, body=%wide.region_11.14_spmd.clone.clone.sunk | while | flops 126194176 | bytes 3312057 | solution.py:86
  461.6 1.4 select_bitcast_fusion.4
  463.0 11.2 %custom-call.33 = f32[2,1,64,64]{2,3,1,0:T(8,128)} custom-call(f32[2,1,64,64]{3,2,1,0:T(8,128)} %select_bitcast_fusion.4), custom_call_target="InvertDiagBlocksLowerTriangular" | custom-call | tf_op jit(solution)/shard_map/jvp(vmap())/while/body/eval_jaxpr/jit(_solve_triangular)/triangular_solve/custom-call.1 | solution.py:57
  474.2 1.8 bitcast_dynamic-update-slice_fusion.22
  477.4 1.7 bitcast_dynamic-update-slice_fusion.24
  488.4 1.4 select_bitcast_fusion.4
  489.8 11.2 %custom-call.33 = f32[2,1,64,64]{2,3,1,0:T(8,128)} custom-call(f32[2,1,64,64]{3,2,1,0:T(8,128)} %select_bitcast_fusion.4), custom_call_target="InvertDiagBlocksLowerTriangular" | custom-call | tf_op jit(solution)/shard_map/jvp(vmap())/while/body/eval_jaxpr/jit(_solve_triangular)/triangular_solve/custom-call.1 | solution.py:57
  501.0 1.8 bitcast_dynamic-update-slice_fusion.22
  504.2 1.7 bitcast_dynamic-update-slice_fusion.24
  515.2 1.4 select_bitcast_fusion.4
  516.6 11.2 %custom-call.33 = f32[2,1,64,64]{2,3,1,0:T(8,128)} custom-call(f32[2,1,64,64]{3,2,1,0:T(8,128)} %select_bitcast_fusion.4), custom_call_target="InvertDiagBlocksLowerTriangular" | custom-call | tf_op jit(solution)/shard_map/jvp(vmap())/while/body/eval_jaxpr/jit(_solve_triangular)/triangular_solve/custom-call.1 | solution.py:57
  527.8 1.8 bitcast_dynamic-update-slice_fusion.22
  531.0 1.7 bitcast_dynamic-update-slice_fusion.24
  542.1 1.4 select_bitcast_fusion.4
  543.5 11.2 %custom-call.33 = f32[2,1,64,64]{2,3,1,0:T(8,128)} custom-call(f32[2,1,64,64]{3,2,1,0:T(8,128)} %select_bitcast_fusion.4), custom_call_target="InvertDiagBlocksLowerTriangular" | custom-call | tf_op jit(solution)/shard_map/jvp(vmap())/while/body/eval_jaxpr/jit(_solve_triangular)/triangular_solve/custom-call.1 | solution.py:57
  554.7 1.8 bitcast_dynamic-update-slice_fusion.22
  557.9 1.7 bitcast_dynamic-update-slice_fusion.24
  569.3 127.3 %while.165 = (s32[]{:T(128)}, f32[2,128,128]{2,1,0:T(8,128)S(1)}, f32[4,2,64,128]{3,2,1,0:T(8,128)}, f32[4,2,64,128]{3,2,1,0:T(8,128)}, f32[4,2,64,128]{3,2,0,1:...) while((s32[]{:T(128)}, f32[2,128,128]{2,1,0:T(8,128)S(1)}, ...), condition=%wide.region_25.27_spmd.clone.clone, body=%wide.region_14.26_spmd.clone.clone.sunk | while | flops 283857920 | bytes 5617773 | solution.py:86
  572.9 9.8 %custom-call.34 = f32[2,1,64,64]{2,3,1,0:T(8,128)S(1)} custom-call(f32[2,1,64,64]{3,2,1,0:T(8,128)S(1)} %select_bitcast_fusion.5), custom_call_target="InvertDiagBlocksLowerTriangular" | custom-call | tf_op jit(solution)/shard_map/transpose(jvp(vmap()))/while/body/eval_jaxpr/jit(_solve_triangular)/triangular_solve | solution.py:57
  591.1 1.7 fusion.375
  594.8 1.8 fusion.380
  604.8 9.8 %custom-call.34 = f32[2,1,64,64]{2,3,1,0:T(8,128)S(1)} custom-call(f32[2,1,64,64]{3,2,1,0:T(8,128)S(1)} %select_bitcast_fusion.5), custom_call_target="InvertDiagBlocksLowerTriangular" | custom-call | tf_op jit(solution)/shard_map/transpose(jvp(vmap()))/while/body/eval_jaxpr/jit(_solve_triangular)/triangular_solve | solution.py:57
  622.9 1.7 fusion.375
  626.6 1.8 fusion.380
  636.6 9.8 %custom-call.34 = f32[2,1,64,64]{2,3,1,0:T(8,128)S(1)} custom-call(f32[2,1,64,64]{3,2,1,0:T(8,128)S(1)} %select_bitcast_fusion.5), custom_call_target="InvertDiagBlocksLowerTriangular" | custom-call | tf_op jit(solution)/shard_map/transpose(jvp(vmap()))/while/body/eval_jaxpr/jit(_solve_triangular)/triangular_solve | solution.py:57
  654.8 1.7 fusion.375
  658.5 1.8 fusion.380
  668.4 9.8 %custom-call.34 = f32[2,1,64,64]{2,3,1,0:T(8,128)S(1)} custom-call(f32[2,1,64,64]{3,2,1,0:T(8,128)S(1)} %select_bitcast_fusion.5), custom_call_target="InvertDiagBlocksLowerTriangular" | custom-call | tf_op jit(solution)/shard_map/transpose(jvp(vmap()))/while/body/eval_jaxpr/jit(_solve_triangular)/triangular_solve | solution.py:57
  686.6 1.7 fusion.375
  690.3 1.8 fusion.380
  701.7 1.5 multiply_reduce_fusion.3
  705.2 1.4 collective-permute-done.1
  707.4 12.7 %all-to-all-start.1 = ((bf16[16,16,512]{2,1,0:T(8,128)(2,1)}), bf16[16,16,512]{2,1,0:T(8,128)(2,1)S(1)}, u32[]{:S(2)}, u32[]{:S(2)}) async-start(bf16[16,16,512]{2,1,0:T(8,128)(2,1)} %bitcast.32), calls=%async_computation.1 | async-start | bytes 524288 | tf_op jit(solution)/shard_map/all_to_all | solution.py:170
  720.8 66.5 %psum.7 = f32[4,512]{1,0:T(4,128)} all-reduce(f32[4,512]{1,0:T(4,128)S(1)} %pad_add_fusion.5), channel_id=1, replica_groups=mesh['ctx'=32,'head'=16] {'ctx'}, use_global_device_ids=true, to_apply=%region_34.36 | all-reduce | flops 2048 | bytes 16384 | tf_op jit(solution)/shard_map/psum | solution.py:173
  (724 shorter events, 346.5 us)
Async XLA Ops:
  7.2 438.4 %copy-start = (f32[2,128,128]{2,1,0:T(8,128)S(1)}, f32[2,128,128]{2,1,0:T(8,128)}, u32[]{:S(2)}) copy-start(f32[2,128,128]{2,1,0:T(8,128)} %param.25) | copy-start | bytes 393220
  8.9 33.1 %all-to-all-start = ((bf16[16,16,512]{2,0,1:T(8,128)(2,1)}), bf16[16,16,512]{2,0,1:T(8,128)(2,1)S(1)}, u32[]{:S(2)}, u32[]{:S(2)}) async-start(bf16[16,16,512]{2,0,1:T(8,128)(2,1)} %bitcast.435), calls=%async_computation | async-start | bytes 524288 | tf_op jit(solution)/shard_map/all_to_all | solution.py:138
  24.1 149.1 %all-gather.9.cloned.1.call-start = ((), (), s32[]{:S(2)}) async-start(), calls=%async_computation.2 | async-start | bytes 4325376 | tf_op jit(solution)/shard_map/all_gather | solution.py:24
  26.3 21.4 %copy-start.8 = (f32[1,512]{1,0:T(1,128)}, f32[1,512]{1,0:T(1,128)S(1)}, u32[]{:S(2)}) copy-start(f32[1,512]{1,0:T(1,128)S(1)} %get-tuple-element.3118) | copy-start | bytes 6148
  26.3 21.4 %copy-start.10 = (f32[1,512]{1,0:T(1,128)}, f32[1,512]{1,0:T(1,128)S(1)}, u32[]{:S(2)}) copy-start(f32[1,512]{1,0:T(1,128)S(1)} %get-tuple-element.3119) | copy-start | bytes 6148
  26.3 21.4 %copy-start.12 = (f32[1,512]{1,0:T(1,128)}, f32[1,512]{1,0:T(1,128)S(1)}, u32[]{:S(2)}) copy-start(f32[1,512]{1,0:T(1,128)S(1)} %get-tuple-element.3120) | copy-start | bytes 6148
  26.4 21.4 %copy-start.14 = (f32[1,512]{1,0:T(1,128)}, f32[1,512]{1,0:T(1,128)S(1)}, u32[]{:S(2)}) copy-start(f32[1,512]{1,0:T(1,128)S(1)} %get-tuple-element.3121) | copy-start | bytes 6148
  42.0 3.4 collective-permute-start
  46.7 0.6 copy-start.18
  46.7 1.8 copy-start.19
  47.3 1.3 copy-start.17
  48.5 66.4 %copy-start.5 = (bf16[256,256]{1,0:T(8,128)(2,1)S(1)}, bf16[256,256]{1,0:T(8,128)(2,1)}, u32[]{:S(2)}) copy-start(bf16[256,256]{1,0:T(8,128)(2,1)} %param.27) | copy-start | bytes 393220
  114.1 2.8 copy-start.2
  114.1 2.8 copy-start.3
  114.9 123.0 %all-gather.11.cloned.1.call-start = ((), (), s32[]{:S(2)}) async-start(), calls=%async_computation.3 | async-start | bytes 4325376 | tf_op jit(solution)/shard_map/all_gather | solution.py:24
  126.2 0.7 copy-start.1
  126.8 191.2 %all-gather.13.cloned.1.call-start = ((), (), s32[]{:S(2)}) async-start(), calls=%async_computation.4 | async-start | bytes 4325376 | tf_op jit(solution)/shard_map/all_gather | solution.py:24
  127.6 238.3 %all-gather.15.cloned.1.call-start = ((), (), s32[]{:S(2)}) async-start(), calls=%async_computation.5 | async-start | bytes 4325376 | tf_op jit(solution)/shard_map/all_gather | solution.py:24
  318.0 47.9 %copy-start.4 = (f32[2,128,128]{2,1,0:T(8,128)}, f32[2,128,128]{2,1,0:T(8,128)S(1)}, u32[]{:S(2)}) copy-start(f32[2,128,128]{2,1,0:T(8,128)S(1)} %get-tuple-element.2004) | copy-start | bytes 393220
  569.3 29.8 %copy-start.7 = (f32[4,2,64]{2,1,0:T(2,128)S(1)}, f32[4,2,64]{2,1,0:T(2,128)}, u32[]{:S(2)}) copy-start(f32[4,2,64]{2,1,0:T(2,128)} %get-tuple-element.4201) | copy-start | bytes 6148 | tf_op jit(solution)/shard_map/transpose(jvp(vmap()))/while
  569.3 30.1 %copy-start.6 = (f32[4,2,64]{2,1,0:T(2,128)S(1)}, f32[4,2,64]{2,1,0:T(2,128)}, u32[]{:S(2)}) copy-start(f32[4,2,64]{2,1,0:T(2,128)} %get-tuple-element.4198) | copy-start | bytes 6148 | tf_op jit(solution)/shard_map/transpose(jvp(vmap()))/while
  601.2 29.8 %copy-start.7 = (f32[4,2,64]{2,1,0:T(2,128)S(1)}, f32[4,2,64]{2,1,0:T(2,128)}, u32[]{:S(2)}) copy-start(f32[4,2,64]{2,1,0:T(2,128)} %get-tuple-element.4201) | copy-start | bytes 6148 | tf_op jit(solution)/shard_map/transpose(jvp(vmap()))/while
  601.2 30.0 %copy-start.6 = (f32[4,2,64]{2,1,0:T(2,128)S(1)}, f32[4,2,64]{2,1,0:T(2,128)}, u32[]{:S(2)}) copy-start(f32[4,2,64]{2,1,0:T(2,128)} %get-tuple-element.4198) | copy-start | bytes 6148 | tf_op jit(solution)/shard_map/transpose(jvp(vmap()))/while
  633.0 29.8 %copy-start.7 = (f32[4,2,64]{2,1,0:T(2,128)S(1)}, f32[4,2,64]{2,1,0:T(2,128)}, u32[]{:S(2)}) copy-start(f32[4,2,64]{2,1,0:T(2,128)} %get-tuple-element.4201) | copy-start | bytes 6148 | tf_op jit(solution)/shard_map/transpose(jvp(vmap()))/while
  633.0 30.0 %copy-start.6 = (f32[4,2,64]{2,1,0:T(2,128)S(1)}, f32[4,2,64]{2,1,0:T(2,128)}, u32[]{:S(2)}) copy-start(f32[4,2,64]{2,1,0:T(2,128)} %get-tuple-element.4198) | copy-start | bytes 6148 | tf_op jit(solution)/shard_map/transpose(jvp(vmap()))/while
  664.8 29.8 %copy-start.7 = (f32[4,2,64]{2,1,0:T(2,128)S(1)}, f32[4,2,64]{2,1,0:T(2,128)}, u32[]{:S(2)}) copy-start(f32[4,2,64]{2,1,0:T(2,128)} %get-tuple-element.4201) | copy-start | bytes 6148 | tf_op jit(solution)/shard_map/transpose(jvp(vmap()))/while
  664.8 30.1 %copy-start.6 = (f32[4,2,64]{2,1,0:T(2,128)S(1)}, f32[4,2,64]{2,1,0:T(2,128)}, u32[]{:S(2)}) copy-start(f32[4,2,64]{2,1,0:T(2,128)} %get-tuple-element.4198) | copy-start | bytes 6148 | tf_op jit(solution)/shard_map/transpose(jvp(vmap()))/while
  696.7 6.5 copy-start.9
  696.7 6.6 copy-start.11
  696.7 6.6 copy-start.13
  696.7 6.6 copy-start.15
  703.5 16.6 %copy-start.16 = (f32[4,2,64]{2,1,0:T(2,128)S(1)}, f32[4,2,64]{2,1,0:T(2,128)}, u32[]{:S(2)}) copy-start(f32[4,2,64]{2,1,0:T(2,128)} %get-tuple-element.2034) | copy-start | bytes 6148
  703.5 83.7 %copy-start.20 = (f32[2,256]{1,0:T(2,128)S(1)}, f32[2,256]{1,0:T(2,128)}, u32[]{:S(2)}) copy-start(f32[2,256]{1,0:T(2,128)} %param.23) | copy-start | bytes 6148
  703.6 3.1 collective-permute-start.1
  707.4 80.5 %all-to-all-start.1 = ((bf16[16,16,512]{2,1,0:T(8,128)(2,1)}), bf16[16,16,512]{2,1,0:T(8,128)(2,1)S(1)}, u32[]{:S(2)}, u32[]{:S(2)}) async-start(bf16[16,16,512]{2,1,0:T(8,128)(2,1)} %bitcast.32), calls=%async_computation.1 | async-start | bytes 524288 | tf_op jit(solution)/shard_map/all_to_all | solution.py:170
Sparse Core Ops, SparseCore 0:
  115.0 58.1 all-gather.8
  176.9 60.8 all-gather.10
  241.0 60.9 all-gather.12
  304.9 60.8 all-gather.14
where the time goes:
time: 802 us; the launch traced here: 795 us
  matrix products  258 us (32%)
  other arithmetic  180 us (22%)
  waiting for transfers between devices  176 us (22%)
  blocking collectives  66.5 us (8%)
  local copies, waits for them, and re-layouts  64.8 us (8%)
  starting transfers between devices  30.8 us (4%)
  between operations  14.3 us (2%)
    all_gather x4, waiting for transfers between devices, prefix(): everything = jax.tree.map(lambda part: lax.all_gather(part, axis), value)  158 us
    another operation x32, other arithmetic, block_step(): solved = jax.scipy.linalg.solve_triangular(system, right_sides, lower=True)  133 us
    dot_general x64, matrix products, compose(): jnp.einsum('hij,hjk->hik', later[0], earlier[1], precision=highest)  79.3 us
    dot_general x64, matrix products, compose(): matrix = jnp.einsum('hij,hjk->hik', later[0], earlier[0], precision=highest)  75.2 us
    psum x1, blocking collectives, on_device(): weight_total = lax.psum(grad_weight, 'ctx')  66.5 us
    dynamic_update_slice x24, other arithmetic, run_head(): (state_end, transit), outputs = lax.scan(block_step, start, pieces)  18.8 us
    dot_general x16, matrix products, block_step(): scores = ratios * jnp.dot(queries, key_feats.T, precision=highest)  18.5 us
    dot_general x20, matrix products, block_step(): jnp.dot(tail_keys.T, update, precision=highest)  17.8 us
  transfers between devices with their start and end apart: 8, of which 5 were waited for; matrix products, arithmetic and copies ran while one was open for 12% of the time, Pallas kernels for 0%

commit v1 on v0

--- a/solution.py
+++ b/solution.py
@@ -170,7 +170,7 @@
     returned = lax.all_to_all(
         own_grad.astype(jnp.bfloat16), "head", split_axis=0, concat_axis=1, tiled=True
     )
-    weight_total = lax.psum(grad_weight, "ctx")
+    weight_total = jnp.sum(lax.all_gather(grad_weight, "ctx"), axis=0)
     return (returned, weight_total, grad_beta, grad_decay)
 
 

time: 802 us -> 764 us (0.953)
  the two profiles are of different devices: /device:TPU:32 before, /device:TPU:1 now
where the time goes in v1:
time: 764 us; the launch traced here: 756 us
  matrix products  258 us (34%)
  other arithmetic  181 us (24%)
  waiting for transfers between devices  170 us (22%)
  local copies, waits for them, and re-layouts  64.8 us (8%)
  starting transfers between devices  39.6 us (5%)
  blocking collectives  24.1 us (3%)
  between operations  14.4 us (2%)
    all_gather x4, waiting for transfers between devices, prefix(): everything = jax.tree.map(lambda part: lax.all_gather(part, axis), value)  155 us
    another operation x32, other arithmetic, block_step(): solved = jax.scipy.linalg.solve_triangular(system, right_sides, lower=True)  133 us
    dot_general x64, matrix products, compose(): jnp.einsum('hij,hjk->hik', later[0], earlier[1], precision=highest)  79.4 us
    dot_general x64, matrix products, compose(): matrix = jnp.einsum('hij,hjk->hik', later[0], earlier[0], precision=highest)  75.2 us
    all_gather x1, blocking collectives, on_device(): weight_total = jnp.sum(lax.all_gather(grad_weight, 'ctx'), axis=0)  24.1 us
    dynamic_update_slice x24, other arithmetic, run_head(): (state_end, transit), outputs = lax.scan(block_step, start, pieces)  18.8 us
    dot_general x16, matrix products, block_step(): scores = ratios * jnp.dot(queries, key_feats.T, precision=highest)  18.5 us
    dot_general x20, matrix products, block_step(): jnp.dot(tail_keys.T, update, precision=highest)  17.8 us
  transfers between devices with their start and end apart: 8, of which 5 were waited for; matrix products, arithmetic and copies ran while one was open for 13% of the time, Pallas kernels for 0%

profile of v1, /device:TPU:1, one launch (start us, length us, event | category | flops | bytes accessed | tf_op | source)
XLA Modules:
  0.0 756.3 jit_solution(11251258442288365357)
XLA Ops:
  7.2 1.7 copy.148
  8.9 15.7 %all-to-all-start = ((bf16[16,16,512]{2,0,1:T(8,128)(2,1)}), bf16[16,16,512]{2,0,1:T(8,128)(2,1)S(1)}, u32[]{:S(2)}, u32[]{:S(2)}) async-start(bf16[16,16,512]{2,0,1:T(8,128)(2,1)} %bitcast.437), calls=%async_computation | async-start | bytes 524288 | tf_op jit(solution)/shard_map/all_to_all | solution.py:138
  26.9 10.9 %all-to-all-done = bf16[16,16,512]{2,0,1:T(8,128)(2,1)S(1)} async-done(((bf16[16,16,512]{2,0,1:T(8,128)(2,1)}), bf16[16,16,512]{2,0,1:T(8,128)(2,1)S(1)}, u32[]{:S(2)}, u32[]{:S(2)}) %all-to-all-start) | async-done | bytes 262176 | tf_op jit(solution)/shard_map/all_to_all | solution.py:138
  37.8 9.3 %collective-permute-start = (bf16[3,512]{1,0:T(4,128)(2,1)S(1)}, bf16[3,512]{1,0:T(4,128)(2,1)S(1)}, u32[]{:S(2)}, u32[]{:S(2)}) collective-permute-start(bf16[3,512]{1,0:T(4,128)(2,1)S(1)} %slice.149), channel_id=1, source_target_pairs={{0,16},{16,32},{32,48},{48,64},{64,80},{80,96},{96,112},{112,128},... | collective-permute-start | bytes 9224 | tf_op jit(solution)/shard_map/ppermute | solution.py:19
  52.3 65.6 %while.169 = (s32[]{:T(128)}, f32[2,128,128]{2,1,0:T(8,128)S(1)}, f32[2,128,128]{2,1,0:T(8,128)S(1)}, f32[4,2,64,128]{3,2,1,0:T(8,128)S(1)}, f32[4,2,64,1]{2,1,3...) while((s32[]{:T(128)}, f32[2,128,128]{2,1,0:T(8,128)S(1)}, ...), condition=%wide.region_4.6_spmd.clone.clone, body=%wide.region_2.5_spmd.clone.clone.sunk | while | flops 176640128 | bytes 2980628 | solution.py:86
  55.3 9.8 %custom-call.35 = f32[2,1,64,64]{2,3,1,0:T(8,128)S(1)} custom-call(f32[2,1,64,64]{3,2,1,0:T(8,128)S(1)} %fusion.420), custom_call_target="InvertDiagBlocksLowerTriangular" | custom-call | tf_op jit(solution)/shard_map/jvp(vmap())/while/body/eval_jaxpr/jit(_solve_triangular)/triangular_solve/custom-call.1 | solution.py:57
  71.6 9.8 %custom-call.35 = f32[2,1,64,64]{2,3,1,0:T(8,128)S(1)} custom-call(f32[2,1,64,64]{3,2,1,0:T(8,128)S(1)} %fusion.420), custom_call_target="InvertDiagBlocksLowerTriangular" | custom-call | tf_op jit(solution)/shard_map/jvp(vmap())/while/body/eval_jaxpr/jit(_solve_triangular)/triangular_solve/custom-call.1 | solution.py:57
  88.0 9.8 %custom-call.35 = f32[2,1,64,64]{2,3,1,0:T(8,128)S(1)} custom-call(f32[2,1,64,64]{3,2,1,0:T(8,128)S(1)} %fusion.420), custom_call_target="InvertDiagBlocksLowerTriangular" | custom-call | tf_op jit(solution)/shard_map/jvp(vmap())/while/body/eval_jaxpr/jit(_solve_triangular)/triangular_solve/custom-call.1 | solution.py:57
  104.4 9.8 %custom-call.35 = f32[2,1,64,64]{2,3,1,0:T(8,128)S(1)} custom-call(f32[2,1,64,64]{3,2,1,0:T(8,128)S(1)} %fusion.420), custom_call_target="InvertDiagBlocksLowerTriangular" | custom-call | tf_op jit(solution)/shard_map/jvp(vmap())/while/body/eval_jaxpr/jit(_solve_triangular)/triangular_solve/custom-call.1 | solution.py:57
  120.7 9.2 %while.166 = (s32[]{:T(128)}, f32[2,128,128]{2,1,0:T(8,128)S(1)}, f32[4,2,1,1]{1,3,2,0:T(1,128)S(1)}, f32[4,2,64,128]{3,2,1,0:T(8,128)S(1)}, f32[4,2,64,1]{2,1,3...) while((s32[]{:T(128)}, f32[2,128,128]{2,1,0:T(8,128)S(1)}, ...), condition=%wide.region_6.8_spmd.clone, body=%wide.region_5.7_spmd.clone.sunk | while | flops 88293376 | bytes 1316019 | solution.py:86
  131.9 42.9 %all-gather.11.cloned.1.call-done = f32[64,128,128]{2,1,0:T(8,128)} async-done(((f32[2,128,128]{2,1,0:T(8,128)}), f32[64,128,128]{2,1,0:T(8,128)}) %all-gather.11.cloned.1.call-update) | async-done | bytes 4194320 | tf_op jit(solution)/shard_map/all_gather | solution.py:24
  174.8 64.6 %all-gather.13.cloned.1.call-done = f32[64,128,128]{2,1,0:T(8,128)} async-done(((f32[2,128,128]{2,1,0:T(8,128)}), f32[64,128,128]{2,1,0:T(8,128)}) %all-gather.13.cloned.1.call-update) | async-done | bytes 4194320 | tf_op jit(solution)/shard_map/all_gather | solution.py:24
  239.5 80.1 %while.167 = (s32[]{:T(128)}, f32[2,128,128]{2,1,0:T(8,128)S(1)}, f32[2,128,128]{2,1,0:T(8,128)S(1)}, s32[]{:T(128)}, f32[32,2,128,128]{3,2,1,0:T(8,128)}, /*ind...) while((s32[]{:T(128)}, f32[2,128,128]{2,1,0:T(8,128)S(1)}, ...), condition=%wide.region_8.10_spmd.clone, body=%wide.region_7.9_spmd.clone.sunk | while | flops 100827144 | bytes 1706674 | solution.py:37
  319.6 47.8 %all-gather.17.cloned.1.call-done = f32[64,128,128]{2,1,0:T(8,128)} async-done(((f32[2,128,128]{2,1,0:T(8,128)}), f32[64,128,128]{2,1,0:T(8,128)}) %all-gather.17.cloned.1.call-update) | async-done | bytes 4194320 | tf_op jit(solution)/shard_map/all_gather | solution.py:24
  367.5 79.6 %while.168 = (s32[]{:T(128)}, f32[2,128,128]{2,1,0:T(8,128)S(1)}, f32[2,128,128]{2,1,0:T(8,128)S(1)}, s32[]{:T(128)}, f32[32,2,128,128]{3,2,1,0:T(8,128)}, /*ind...) while((s32[]{:T(128)}, f32[2,128,128]{2,1,0:T(8,128)S(1)}, f32[2,128,128]{2,1,0:T(8,128)S(1)}, ...), condition=%wide.region_10.12_spmd.clone, body=%wide.region_9.11_spmd.clone.sunk | while | flops 100827136 | bytes 1706612 | solution.py:37
  459.6 107.3 %while.164 = (s32[]{:T(128)}, f32[2,128,128]{2,1,0:T(8,128)S(1)}, f32[4,2,64,64]{3,2,1,0:T(8,128)}, f32[4,2,128,64]{2,3,1,0:T(8,128)}, f32[4,2,64,64]{3,2,1,0:T(...) while((s32[]{:T(128)}, f32[2,128,128]{2,1,0:T(8,128)S(1)}, ...), condition=%wide.region_13.15_spmd.clone.clone, body=%wide.region_11.14_spmd.clone.clone.sunk | while | flops 126194176 | bytes 3312057 | solution.py:86
  464.6 11.2 %custom-call.33 = f32[2,1,64,64]{2,3,1,0:T(8,128)} custom-call(f32[2,1,64,64]{3,2,1,0:T(8,128)} %select_bitcast_fusion.4), custom_call_target="InvertDiagBlocksLowerTriangular" | custom-call | tf_op jit(solution)/shard_map/jvp(vmap())/while/body/eval_jaxpr/jit(_solve_triangular)/triangular_solve/custom-call.1 | solution.py:57
  475.8 1.8 bitcast_dynamic-update-slice_fusion.22
  479.0 1.7 bitcast_dynamic-update-slice_fusion.24
  490.0 1.4 select_bitcast_fusion.4
  491.4 11.2 %custom-call.33 = f32[2,1,64,64]{2,3,1,0:T(8,128)} custom-call(f32[2,1,64,64]{3,2,1,0:T(8,128)} %select_bitcast_fusion.4), custom_call_target="InvertDiagBlocksLowerTriangular" | custom-call | tf_op jit(solution)/shard_map/jvp(vmap())/while/body/eval_jaxpr/jit(_solve_triangular)/triangular_solve/custom-call.1 | solution.py:57
  502.6 1.8 bitcast_dynamic-update-slice_fusion.22
  505.8 1.7 bitcast_dynamic-update-slice_fusion.24
  518.3 11.2 %custom-call.33 = f32[2,1,64,64]{2,3,1,0:T(8,128)} custom-call(f32[2,1,64,64]{3,2,1,0:T(8,128)} %select_bitcast_fusion.4), custom_call_target="InvertDiagBlocksLowerTriangular" | custom-call | tf_op jit(solution)/shard_map/jvp(vmap())/while/body/eval_jaxpr/jit(_solve_triangular)/triangular_solve/custom-call.1 | solution.py:57
  529.4 1.8 bitcast_dynamic-update-slice_fusion.22
  532.6 1.7 bitcast_dynamic-update-slice_fusion.24
  543.7 1.4 select_bitcast_fusion.4
  545.1 11.2 %custom-call.33 = f32[2,1,64,64]{2,3,1,0:T(8,128)} custom-call(f32[2,1,64,64]{3,2,1,0:T(8,128)} %select_bitcast_fusion.4), custom_call_target="InvertDiagBlocksLowerTriangular" | custom-call | tf_op jit(solution)/shard_map/jvp(vmap())/while/body/eval_jaxpr/jit(_solve_triangular)/triangular_solve/custom-call.1 | solution.py:57
  556.3 1.8 bitcast_dynamic-update-slice_fusion.22
  559.5 1.7 bitcast_dynamic-update-slice_fusion.24
  570.9 127.3 %while.165 = (s32[]{:T(128)}, f32[2,128,128]{2,1,0:T(8,128)S(1)}, f32[4,2,64,128]{3,2,1,0:T(8,128)}, f32[4,2,64,128]{3,2,1,0:T(8,128)}, f32[4,2,64,128]{3,2,0,1:...) while((s32[]{:T(128)}, f32[2,128,128]{2,1,0:T(8,128)S(1)}, ...), condition=%wide.region_25.27_spmd.clone.clone, body=%wide.region_14.26_spmd.clone.clone.sunk | while | flops 283857920 | bytes 5617773 | solution.py:86
  574.5 9.8 %custom-call.34 = f32[2,1,64,64]{2,3,1,0:T(8,128)S(1)} custom-call(f32[2,1,64,64]{3,2,1,0:T(8,128)S(1)} %select_bitcast_fusion.5), custom_call_target="InvertDiagBlocksLowerTriangular" | custom-call | tf_op jit(solution)/shard_map/transpose(jvp(vmap()))/while/body/eval_jaxpr/jit(_solve_triangular)/triangular_solve | solution.py:57
  592.7 1.7 fusion.375
  596.4 1.8 fusion.380
  606.4 9.8 %custom-call.34 = f32[2,1,64,64]{2,3,1,0:T(8,128)S(1)} custom-call(f32[2,1,64,64]{3,2,1,0:T(8,128)S(1)} %select_bitcast_fusion.5), custom_call_target="InvertDiagBlocksLowerTriangular" | custom-call | tf_op jit(solution)/shard_map/transpose(jvp(vmap()))/while/body/eval_jaxpr/jit(_solve_triangular)/triangular_solve | solution.py:57
  624.5 1.7 fusion.375
  628.2 1.8 fusion.380
  638.2 9.8 %custom-call.34 = f32[2,1,64,64]{2,3,1,0:T(8,128)S(1)} custom-call(f32[2,1,64,64]{3,2,1,0:T(8,128)S(1)} %select_bitcast_fusion.5), custom_call_target="InvertDiagBlocksLowerTriangular" | custom-call | tf_op jit(solution)/shard_map/transpose(jvp(vmap()))/while/body/eval_jaxpr/jit(_solve_triangular)/triangular_solve | solution.py:57
  656.4 1.7 fusion.375
  660.1 1.8 fusion.380
  670.0 9.8 %custom-call.34 = f32[2,1,64,64]{2,3,1,0:T(8,128)S(1)} custom-call(f32[2,1,64,64]{3,2,1,0:T(8,128)S(1)} %select_bitcast_fusion.5), custom_call_target="InvertDiagBlocksLowerTriangular" | custom-call | tf_op jit(solution)/shard_map/transpose(jvp(vmap()))/while/body/eval_jaxpr/jit(_solve_triangular)/triangular_solve | solution.py:57
  688.2 1.7 fusion.375
  691.9 1.8 fusion.380
  703.4 1.5 multiply_reduce_fusion.3
  705.2 2.2 collective-permute-start.1
  707.7 2.4 collective-permute-done.1
  710.9 12.0 %all-to-all-start.1 = ((bf16[16,16,512]{2,1,0:T(8,128)(2,1)}), bf16[16,16,512]{2,1,0:T(8,128)(2,1)S(1)}, u32[]{:S(2)}, u32[]{:S(2)}) async-start(bf16[16,16,512]{2,1,0:T(8,128)(2,1)} %bitcast.32), calls=%async_computation.1 | async-start | bytes 524288 | tf_op jit(solution)/shard_map/all_to_all | solution.py:170
  723.7 24.1 %all-gather.5 = f32[32,4,512]{2,1,0:T(4,128)S(1)} all-gather(f32[1,4,512]{2,1,0:T(4,128)S(1)} %add_bitcast_fusion), channel_id=6, replica_groups=mesh['ctx'=32,'head'=16] {'ctx'}, dimensions={0}, use_global_device_ids=true | all-gather | bytes 270336 | tf_op jit(solution)/shard_map/all_gather | solution.py:173
  (725 shorter events, 347.5 us)
Async XLA Ops:
  7.2 440.0 %copy-start = (f32[2,128,128]{2,1,0:T(8,128)S(1)}, f32[2,128,128]{2,1,0:T(8,128)}, u32[]{:S(2)}) copy-start(f32[2,128,128]{2,1,0:T(8,128)} %param.25) | copy-start | bytes 393220
  8.9 28.9 %all-to-all-start = ((bf16[16,16,512]{2,0,1:T(8,128)(2,1)}), bf16[16,16,512]{2,0,1:T(8,128)(2,1)S(1)}, u32[]{:S(2)}, u32[]{:S(2)}) async-start(bf16[16,16,512]{2,0,1:T(8,128)(2,1)} %bitcast.437), calls=%async_computation | async-start | bytes 524288 | tf_op jit(solution)/shard_map/all_to_all | solution.py:138
  24.6 150.2 %all-gather.11.cloned.1.call-start = ((), (), s32[]{:S(2)}) async-start(), calls=%async_computation.2 | async-start | bytes 4325376 | tf_op jit(solution)/shard_map/all_gather | solution.py:24
  26.9 24.6 %copy-start.8 = (f32[1,512]{1,0:T(1,128)}, f32[1,512]{1,0:T(1,128)S(1)}, u32[]{:S(2)}) copy-start(f32[1,512]{1,0:T(1,128)S(1)} %get-tuple-element.3118) | copy-start | bytes 6148
  26.9 24.6 %copy-start.10 = (f32[1,512]{1,0:T(1,128)}, f32[1,512]{1,0:T(1,128)S(1)}, u32[]{:S(2)}) copy-start(f32[1,512]{1,0:T(1,128)S(1)} %get-tuple-element.3119) | copy-start | bytes 6148
  26.9 24.6 %copy-start.12 = (f32[1,512]{1,0:T(1,128)}, f32[1,512]{1,0:T(1,128)S(1)}, u32[]{:S(2)}) copy-start(f32[1,512]{1,0:T(1,128)S(1)} %get-tuple-element.3120) | copy-start | bytes 6148
  26.9 24.6 %copy-start.14 = (f32[1,512]{1,0:T(1,128)}, f32[1,512]{1,0:T(1,128)S(1)}, u32[]{:S(2)}) copy-start(f32[1,512]{1,0:T(1,128)S(1)} %get-tuple-element.3121) | copy-start | bytes 6148
  37.8 11.3 %collective-permute-start = (bf16[3,512]{1,0:T(4,128)(2,1)S(1)}, bf16[3,512]{1,0:T(4,128)(2,1)S(1)}, u32[]{:S(2)}, u32[]{:S(2)}) collective-permute-start(bf16[3,512]{1,0:T(4,128)(2,1)S(1)} %slice.149), channel_id=1, source_target_pairs={{0,16},{16,32},{32,48},{48,64},{64,80},{80,96},{96,112},{112,128},... | collective-permute-start | bytes 9224 | tf_op jit(solution)/shard_map/ppermute | solution.py:19
  50.5 0.6 copy-start.18
  50.5 1.8 copy-start.19
  51.0 1.3 copy-start.17
  52.3 66.4 %copy-start.5 = (bf16[256,256]{1,0:T(8,128)(2,1)S(1)}, bf16[256,256]{1,0:T(8,128)(2,1)}, u32[]{:S(2)}) copy-start(bf16[256,256]{1,0:T(8,128)(2,1)} %param.27) | copy-start | bytes 393220
  117.9 2.8 copy-start.2
  117.9 2.8 copy-start.3
  118.7 120.8 %all-gather.13.cloned.1.call-start = ((), (), s32[]{:S(2)}) async-start(), calls=%async_computation.3 | async-start | bytes 4325376 | tf_op jit(solution)/shard_map/all_gather | solution.py:24
  129.9 0.7 copy-start.1
  130.6 189.0 %all-gather.15.cloned.1.call-start = ((), (), s32[]{:S(2)}) async-start(), calls=%async_computation.4 | async-start | bytes 4325376 | tf_op jit(solution)/shard_map/all_gather | solution.py:24
  131.4 236.1 %all-gather.17.cloned.1.call-start = ((), (), s32[]{:S(2)}) async-start(), calls=%async_computation.5 | async-start | bytes 4325376 | tf_op jit(solution)/shard_map/all_gather | solution.py:24
  319.6 47.9 %copy-start.4 = (f32[2,128,128]{2,1,0:T(8,128)}, f32[2,128,128]{2,1,0:T(8,128)S(1)}, u32[]{:S(2)}) copy-start(f32[2,128,128]{2,1,0:T(8,128)S(1)} %get-tuple-element.2004) | copy-start | bytes 393220
  570.9 29.8 %copy-start.7 = (f32[4,2,64]{2,1,0:T(2,128)S(1)}, f32[4,2,64]{2,1,0:T(2,128)}, u32[]{:S(2)}) copy-start(f32[4,2,64]{2,1,0:T(2,128)} %get-tuple-element.4201) | copy-start | bytes 6148 | tf_op jit(solution)/shard_map/transpose(jvp(vmap()))/while
  570.9 30.1 %copy-start.6 = (f32[4,2,64]{2,1,0:T(2,128)S(1)}, f32[4,2,64]{2,1,0:T(2,128)}, u32[]{:S(2)}) copy-start(f32[4,2,64]{2,1,0:T(2,128)} %get-tuple-element.4198) | copy-start | bytes 6148 | tf_op jit(solution)/shard_map/transpose(jvp(vmap()))/while
  602.8 29.8 %copy-start.7 = (f32[4,2,64]{2,1,0:T(2,128)S(1)}, f32[4,2,64]{2,1,0:T(2,128)}, u32[]{:S(2)}) copy-start(f32[4,2,64]{2,1,0:T(2,128)} %get-tuple-element.4201) | copy-start | bytes 6148 | tf_op jit(solution)/shard_map/transpose(jvp(vmap()))/while
  602.8 30.0 %copy-start.6 = (f32[4,2,64]{2,1,0:T(2,128)S(1)}, f32[4,2,64]{2,1,0:T(2,128)}, u32[]{:S(2)}) copy-start(f32[4,2,64]{2,1,0:T(2,128)} %get-tuple-element.4198) | copy-start | bytes 6148 | tf_op jit(solution)/shard_map/transpose(jvp(vmap()))/while
  634.6 29.8 %copy-start.7 = (f32[4,2,64]{2,1,0:T(2,128)S(1)}, f32[4,2,64]{2,1,0:T(2,128)}, u32[]{:S(2)}) copy-start(f32[4,2,64]{2,1,0:T(2,128)} %get-tuple-element.4201) | copy-start | bytes 6148 | tf_op jit(solution)/shard_map/transpose(jvp(vmap()))/while
  634.6 30.0 %copy-start.6 = (f32[4,2,64]{2,1,0:T(2,128)S(1)}, f32[4,2,64]{2,1,0:T(2,128)}, u32[]{:S(2)}) copy-start(f32[4,2,64]{2,1,0:T(2,128)} %get-tuple-element.4198) | copy-start | bytes 6148 | tf_op jit(solution)/shard_map/transpose(jvp(vmap()))/while
  666.4 29.8 %copy-start.7 = (f32[4,2,64]{2,1,0:T(2,128)S(1)}, f32[4,2,64]{2,1,0:T(2,128)}, u32[]{:S(2)}) copy-start(f32[4,2,64]{2,1,0:T(2,128)} %get-tuple-element.4201) | copy-start | bytes 6148 | tf_op jit(solution)/shard_map/transpose(jvp(vmap()))/while
  666.4 30.1 %copy-start.6 = (f32[4,2,64]{2,1,0:T(2,128)S(1)}, f32[4,2,64]{2,1,0:T(2,128)}, u32[]{:S(2)}) copy-start(f32[4,2,64]{2,1,0:T(2,128)} %get-tuple-element.4198) | copy-start | bytes 6148 | tf_op jit(solution)/shard_map/transpose(jvp(vmap()))/while
  698.3 6.5 copy-start.9
  698.3 6.6 copy-start.11
  698.3 6.6 copy-start.13
  698.3 6.6 copy-start.15
  705.1 17.9 %copy-start.16 = (f32[4,2,64]{2,1,0:T(2,128)S(1)}, f32[4,2,64]{2,1,0:T(2,128)}, u32[]{:S(2)}) copy-start(f32[4,2,64]{2,1,0:T(2,128)} %get-tuple-element.2034) | copy-start | bytes 6148
  705.2 43.3 %copy-start.20 = (f32[2,256]{1,0:T(2,128)S(1)}, f32[2,256]{1,0:T(2,128)}, u32[]{:S(2)}) copy-start(f32[2,256]{1,0:T(2,128)} %param.23) | copy-start | bytes 6148
  705.2 5.0 collective-permute-start.1
  710.9 38.1 %all-to-all-start.1 = ((bf16[16,16,512]{2,1,0:T(8,128)(2,1)}), bf16[16,16,512]{2,1,0:T(8,128)(2,1)S(1)}, u32[]{:S(2)}, u32[]{:S(2)}) async-start(bf16[16,16,512]{2,1,0:T(8,128)(2,1)} %bitcast.32), calls=%async_computation.1 | async-start | bytes 524288 | tf_op jit(solution)/shard_map/all_to_all | solution.py:170
Sparse Core Ops, SparseCore 0:
  118.8 56.0 all-gather.10
  178.6 60.8 all-gather.12
  242.6 60.9 all-gather.14
  306.6 60.8 all-gather.16
